TPU v7x, 32 devices: a whole 2x2x4 slice. The times are simulated.
32 devices in a mesh: mem: 2 (over x), gy: 4 (over z), gx: 4 (over y, core).
Axes of the slice: x: 2, y: 2, z: 4, core: 2. Of those that a mesh axis runs over, the one named last changes fastest.
Arguments:
- alpha: float32 [16, 32, 64, 512], P('mem', None, 'gy', 'gx'), may hold values from -4 to 4
- perturb: bfloat16 [16, 4, 32, 64, 512], P('mem', None, None, 'gy', 'gx'), may hold values from -6 to 6
- chi: float32 [4, 32, 64, 512], P(None, None, 'gy', 'gx'), may hold values from -4 to 4
- kappa: float32 [64, 512], P('gy', 'gx'), may hold values from 0.05 to 0.24
- vert_bounds: int32 [2, 32], replicated, may hold values from 0 to 31, as said below
- static_vert: float32 [4, 32, 32], replicated, may hold values from -1 to 1
- fine_owner: int32 [16, 2], P(('gy', 'gx')), may hold values from 0 to 1, each once within a row
- obs_stencil: int32 [32768], P(('mem', 'gy', 'gx')), may hold values from 0 to 959
- obs_weight: float32 [4, 32768], P(None, ('mem', 'gy', 'gx')), may hold values from 0.05 to 0.5
- background: bfloat16 [32768, 128], P(('mem', 'gy', 'gx')), may hold values from -6 to 6
- observed: float32 [8, 32768], P(None, ('mem', 'gy', 'gx')), may hold values from -6 to 6
- inv_var: float32 [8, 32768], P(None, ('mem', 'gy', 'gx')), may hold values from 2 to 32
- jacobian: float32 [8, 128], replicated, may hold values from -0.5 to 0.5
- obs_count: int32 [32], P(('mem', 'gy', 'gx')), may hold values from 256 to 1024, as said below
Outputs:
- grad_alpha: float32 [16, 32, 64, 512], P('mem', None, 'gy', 'gx')
- grad_chi: float32 [4, 32, 64, 512], P(None, None, 'gy', 'gx')
Inputs may be any that keep to these rules, and one draw needn't show every extreme that they name: `vert_bounds`: row 0 holds each level's lowest and row 1 its highest coupled level; level l lies between both inclusive, and each lies 1 to 4 levels from l unless cut at the ends of the column. `obs_count`: observations below this count in a device's block are live; some device has exactly 1024 and some exactly 256.
All inputs are finite; a program needn't handle non-finite values.
Results may differ from a plain program's by a relative error of at most 0.00099.
Values may be sent and summed in bfloat16 or wider, within the bound.
A program may use at most 128 MiB of HBM per device.

v0:
```python
import math
import jax
import jax.numpy as jnp
from jax import lax
from jax.sharding import PartitionSpec as P

NDIFF = 4
ensemble_weight = 0.8
static_weight = 0.6
vertical_scale = 2.0
highest = lax.Precision.HIGHEST


def padded_2(cells, sides, width):
    for axis, dim in sides:
        count = lax.axis_size(axis)
        head = lax.slice_in_dim(cells, 0, width, axis=dim)
        tail = lax.slice_in_dim(cells, cells.shape[dim] - width, cells.shape[dim], axis=dim)
        cells = jnp.concatenate(
            [
                lax.ppermute(tail, axis, [(i, (i + 1) % count) for i in range(count)]),
                cells,
                lax.ppermute(head, axis, [((i + 1) % count, i) for i in range(count)]),
            ],
            axis=dim,
        )
    return cells


def shifted(value, axis, steps):
    count = lax.axis_size(axis)
    pairs = [(source, (source + steps) % count) for source in range(count)]
    return lax.ppermute(value, axis, pairs)


def vertical_matrix(vert_bounds, levels):
    row_level = lax.broadcasted_iota(jnp.int32, (levels, levels), 0)
    col_level = lax.broadcasted_iota(jnp.int32, (levels, levels), 1)
    inside = (col_level >= vert_bounds[0][:, None]) & (col_level <= vert_bounds[1][:, None])
    distance = jnp.abs(row_level - col_level).astype(jnp.float32)
    return jnp.where(inside, jnp.exp(-distance / vertical_scale), jnp.zeros_like(distance))


def deep_pad(values, margin):
    padded = padded_2(values, (("gy", 2), ("gx", 3)), margin)
    row_place = lax.axis_index("gy")
    upper_rows = jnp.flip(padded[:, :, margin : 2 * margin], axis=2)
    lower_rows = jnp.flip(padded[:, :, -2 * margin : -margin], axis=2)
    north_fixed = jnp.concatenate([upper_rows, padded[:, :, margin:]], axis=2)
    padded = jnp.where(row_place == 0, north_fixed, padded)
    south_fixed = jnp.concatenate([padded[:, :, :-margin], lower_rows], axis=2)
    return jnp.where(row_place == lax.axis_size("gy") - 1, south_fixed, padded)


def stencil_of(padded):
    center = padded[:, :, 1:-1, 1:-1]
    return (
        padded[:, :, :-2, 1:-1]
        + padded[:, :, 2:, 1:-1]
        + padded[:, :, 1:-1, :-2]
        + padded[:, :, 1:-1, 2:]
        - 4.0 * center
    )


def sweep_forward(padded, kappa_pad):
    for repeat in range(NDIFF):
        stencil_sum = stencil_of(padded)
        kappa_pad = kappa_pad[:, :, 1:-1, 1:-1]
        padded = padded[:, :, 1:-1, 1:-1] + kappa_pad * stencil_sum
    return padded


def sweep_adjoint(padded, kappa_pad):
    for repeat in range(NDIFF):
        stencil_sum = stencil_of(kappa_pad * padded)
        kappa_pad = kappa_pad[:, :, 1:-1, 1:-1]
        padded = padded[:, :, 1:-1, 1:-1] + stencil_sum
    return padded


def to_cells(values, column_width):
    return jnp.transpose(values.reshape(column_width, values.shape[2], values.shape[3]), (1, 2, 0))


def from_cells(cell_table, variables, levels):
    return jnp.transpose(cell_table, (2, 0, 1)).reshape(
        variables, levels, cell_table.shape[0], cell_table.shape[1]
    )


def extend_east(cell_table, rim_cols):
    rim_part = shifted(cell_table[:, :rim_cols], "gx", -1)
    return jnp.concatenate([cell_table, rim_part], axis=1)


def fold_east(wide_grad, tile_cols, rim_cols):
    from_west = shifted(wide_grad[:, tile_cols:], "gx", 1)
    head_cols = wide_grad[:, :rim_cols] + from_west
    return jnp.concatenate([head_cols, wide_grad[:, rim_cols:tile_cols]], axis=1)


def observe(region, obs_stencil, obs_weight, background, observed, inv_var, jacobian, obs_count):
    row_count, region_cols, column_width = region.shape
    band_size = region_cols - 1
    slot_table = region.reshape(row_count * region_cols, column_width)
    anchor_row = obs_stencil // band_size
    anchor_col = obs_stencil % band_size
    cell_index = [
        (anchor_row + corner // 2) * region_cols + anchor_col + corner % 2 for corner in range(4)
    ]
    increment_obs = jnp.zeros(background.shape, jnp.float32)
    for corner in range(4):
        picked = jnp.take(slot_table, cell_index[corner], axis=0).astype(jnp.float32)
        increment_obs = increment_obs + obs_weight[corner][:, None] * picked
    bent = jnp.tanh(background.astype(jnp.float32) + increment_obs)
    modeled = jnp.einsum("cv,ov->co", jacobian, bent, precision=highest)
    position = lax.broadcasted_iota(jnp.int32, modeled.shape, 1)
    misfit = jnp.where(
        position < obs_count[0], (modeled - observed) * inv_var, jnp.zeros_like(modeled)
    )
    state_grad = (1.0 - bent * bent) * jnp.einsum("co,cv->ov", misfit, jacobian, precision=highest)
    returned = jnp.zeros(slot_table.shape, jnp.float32)
    for corner in range(4):
        returned = returned.at[cell_index[corner]].add(obs_weight[corner][:, None] * state_grad)
    return returned.reshape(row_count, region_cols, column_width)


def body(
    alpha,
    perturb,
    chi,
    kappa,
    vert_bounds,
    static_vert,
    fine_owner,
    obs_stencil,
    obs_weight,
    background,
    observed,
    inv_var,
    jacobian,
    obs_count,
):
    members, levels, tile_rows, tile_cols = alpha.shape
    variables = perturb.shape[1]
    column_width = variables * levels
    member_groups = lax.axis_size("mem")
    band_width = tile_cols // member_groups
    shift_cols = band_width // 2
    rim_cols = shift_cols + 1
    member_group = lax.axis_index("mem")
    owner_row = fine_owner[0]
    band_ids = lax.broadcasted_iota(jnp.int32, (member_groups, member_groups), 1)
    own_band = jnp.sum(
        jnp.where(owner_row == member_group, band_ids[0], jnp.zeros_like(band_ids[0]))
    )
    region_offsets = lax.broadcasted_iota(jnp.int32, (band_width + 1,), 0)
    ens_scale = ensemble_weight / math.sqrt(members * member_groups - 1)
    vertical = vertical_matrix(vert_bounds, levels)
    spread = jnp.einsum("lm,kmyx->klyx", vertical, alpha, precision=highest)
    kappa_pad = deep_pad(kappa[None, None], NDIFF)
    spread = sweep_forward(deep_pad(spread, NDIFF), kappa_pad)
    partial_sum = jnp.sum(perturb.astype(jnp.float32) * spread[:, None], axis=0)
    member_total = lax.psum(partial_sum, "mem")
    static = jnp.einsum("vlm,vmyx->vlyx", static_vert, chi, precision=highest)
    increment = (ens_scale * member_total + static_weight * static).astype(jnp.bfloat16)
    widened = extend_east(to_cells(increment, column_width), rim_cols)
    own_cols = own_band * band_width + shift_cols + region_offsets
    region = jnp.take(widened, own_cols, axis=1)
    region_grad = observe(
        region, obs_stencil, obs_weight, background, observed, inv_var, jacobian, obs_count
    )
    wide_grad = jnp.zeros(widened.shape, jnp.float32).at[:, own_cols].add(region_grad)
    tile_grad = fold_east(wide_grad, tile_cols, rim_cols)
    gradient_cells = lax.psum(tile_grad, "mem")
    gradient = from_cells(gradient_cells, variables, levels)
    grad_chi = chi + static_weight * jnp.einsum(
        "vlm,vlyx->vmyx", static_vert, gradient, precision=highest
    )
    back_spread = ens_scale * jnp.sum(perturb.astype(jnp.float32) * gradient[None], axis=1)
    back_spread = sweep_adjoint(deep_pad(back_spread, NDIFF), kappa_pad)
    grad_alpha = alpha + jnp.einsum("lm,klyx->kmyx", vertical, back_spread, precision=highest)
    return (grad_alpha, grad_chi)


def solution(mesh):
    in_specs = (
        P("mem", None, "gy", "gx"),
        P("mem", None, None, "gy", "gx"),
        P(None, None, "gy", "gx"),
        P("gy", "gx"),
        P(),
        P(),
        P(("gy", "gx"), None),
        P(("mem", "gy", "gx")),
        P(None, ("mem", "gy", "gx")),
        P(("mem", "gy", "gx"), None),
        P(None, ("mem", "gy", "gx")),
        P(None, ("mem", "gy", "gx")),
        P(),
        P(("mem", "gy", "gx")),
    )
    out_specs = (P("mem", None, "gy", "gx"), P(None, None, "gy", "gx"))
    return jax.shard_map(body, mesh=mesh, in_specs=in_specs, out_specs=out_specs, check_vma=False)
```

profile of v0, /device:TPU:0, one launch (start us, length us, event | category | flops | bytes accessed | tf_op | source)
XLA Modules:
  0.0 408.9 jit_solution(9989891320124790640)
XLA Ops:
  8.0 3.1 collective-permute-start.4
  11.0 2.0 collective-permute-start.5
  13.8 3.9 fusion.28
  18.7 3.8 collective-permute-start.1
  23.4 1.7 collective-permute-start.7
  27.2 8.3 %collective-permute-done = f32[8,32,4,128]{3,1,2,0:T(8,128)S(1)} collective-permute-done((f32[8,32,4,128]{3,1,2,0:T(8,128)}, f32[8,32,4,128]{3,1,2,0:T(8,128)S(1)}, u32[]{:S(2)}, u32[]{:S(2)}) %collective-permute-start) | collective-permute-done | bytes 524320 | tf_op jit(solution)/shard_map/ppermute | solution.py:21
  35.5 8.0 %collective-permute-done.1 = f32[8,32,4,128]{3,1,2,0:T(8,128)S(1)} collective-permute-done((f32[8,32,4,128]{3,1,2,0:T(8,128)}, f32[8,32,4,128]{3,1,2,0:T(8,128)S(1)}, u32[]{:S(2)}, u32[]{:S(2)}) %collective-permute-start.1) | collective-permute-done | bytes 524320 | tf_op jit(solution)/shard_map/ppermute | solution.py:23
  43.9 3.7 fusion.88
  47.6 3.4 copy.52
  51.0 3.4 copy.53
  55.4 10.8 %collective-permute-done.2 = f32[8,32,24,4]{1,2,3,0:T(8,128)} collective-permute-done((f32[8,32,24,4]{1,2,3,0:T(8,128)}, f32[8,32,24,4]{1,2,3,0:T(8,128)}, u32[]{:S(2)}, u32[]{:S(2)}) %collective-permute-start.2) | collective-permute-done | bytes 98336 | tf_op jit(solution)/shard_map/ppermute | solution.py:21
  66.2 3.4 copy.54
  69.6 3.4 copy.55
  72.9 5.7 %pad_maximum_fusion = f32[8,32,24,136]{3,1,2,0:T(8,128)S(1)} fusion(f32[8,32,24,4]{3,1,2,0:T(8,128)} %copy.55, f32[8,32,4,128]{3,1,2,0:T(8,128)S(1)} %collective-permute-done.1, f32[8,32,16,128]{3,1,2,0:T(8,128)S(1)} %fusion.28, f32[8,32,4,128]{3,1,2,0:T(8,128)S(1)} %collective-permute-done, f32[8,32,24,4]{3,1,2,0:T(8,128)} %copy.54), kind=kLoop, calls=%fused_computation.14 | loop fusion | flops 3342336 | bytes 6684672 | tf_op jit(solution)/shard_map/concatenate | solution.py:19
  80.1 2.8 slice.361
  82.9 2.3 rev.21
  85.2 2.3 rev.20
  87.5 6.6 %maximum_select_fusion = f32[8,32,24,136]{3,1,2,0:T(8,128)S(1)} fusion(f32[8,32,20,136]{3,1,2,0:T(8,128)} %slice.361, f32[8,32,4,136]{3,1,2,0:T(8,128)} %rev.20, pred[]{:T(512)S(6)} %eq.20, f32[8,32,24,4]{3,1,2,0:T(8,128)} %copy.55, f32[8,32,4,128]{3,1,2,0:T(8,128)S(1)} %collective-permute-done.1, f32[8,32,16,128]{3,1,2,0:T(8,128)S(1)} %fusion.28, ...), kind=kLoop, calls=%fused_computation.15 | loop fusion | flops 5013504 | bytes 10027009 | tf_op jit(solution)/shard_map/jit(_where)/select_n | solution.py:50
  94.1 2.6 copy-done.2
  96.8 2.8 slice.362
  99.6 5.9 %maximum_select_fusion.1 = f32[8,32,24,136]{3,1,2,0:T(8,128)S(1)} fusion(f32[8,32,24,136]{3,1,2,0:T(8,128)} %copy-done.2, f32[8,32,4,136]{3,1,2,0:T(8,128)S(1)} %copy-done.7, f32[8,32,20,136]{3,1,2,0:T(8,128)} %slice.362, pred[]{:T(512)S(6)} %eq.19), kind=kLoop, calls=%fused_computation.16 | loop fusion | flops 1671168 | bytes 10027009 | tf_op jit(solution)/shard_map/jit(_where)/select_n | solution.py:52
  105.5 6.1 %fusion.6 = f32[8,32,22,134]{3,1,2,0:T(8,128)S(1)} fusion(f32[8,32,24,136]{3,1,2,0:T(8,128)S(1)} %maximum_select_fusion.1, f32[22,134]{1,0:T(8,128)S(1)} %slice_bitcast_fusion.2), kind=kLoop, calls=%fused_computation.29 | loop fusion | flops 5282816 | bytes 18124304 | tf_op jit(solution)/shard_map/add | solution.py:70
  111.6 5.7 %fusion.11 = f32[8,32,20,132]{3,1,2,0:T(8,128)S(1)} fusion(f32[8,32,22,134]{3,1,2,0:T(8,128)S(1)} %fusion.6, f32[20,132]{1,0:T(8,128)S(1)} %slice_bitcast_fusion.1), kind=kLoop, calls=%fused_computation.41 | loop fusion | flops 4730880 | bytes 16230720 | tf_op jit(solution)/shard_map/add | solution.py:70
  117.3 5.0 %fusion.16 = f32[8,32,18,130]{3,1,2,0:T(8,128)S(1)} fusion(f32[8,32,20,132]{3,1,2,0:T(8,128)S(1)} %fusion.11, f32[18,130]{1,0:T(8,128)S(1)} %slice_bitcast_fusion), kind=kLoop, calls=%fused_computation.53 | loop fusion | flops 4193280 | bytes 14386320 | tf_op jit(solution)/shard_map/add | solution.py:70
  122.4 2.2 fusion.25
  129.8 38.5 %all-reduce.3.cloned.1.call-done = f32[4,32,16,128]{3,1,2,0:T(8,128)} async-done(((f32[4,32,16,128]{3,1,2,0:T(8,128)}), f32[4,32,16,128]{3,1,2,0:T(8,128)}) %all-reduce.3.cloned.1.call-update) | async-done | bytes 1048592 | tf_op jit(solution)/shard_map/psum | solution.py:165
  168.3 2.5 fusion.36
  173.0 2.4 collective-permute-done.8
  176.5 3.2 gather_fusion.4
  179.7 3.2 gather_fusion.3
  183.0 3.2 gather_fusion.2
  186.2 3.2 gather_fusion.1
  192.4 6.7 %scatter_custom_fusion = f32[1040,128]{1,0:T(8,128)S(1)} fusion(s32[1024]{0:T(1024)S(1)} %get-tuple-element.64, f32[1024,128]{1,0:T(8,128)S(1)} %convolution_multiply_fusion.2, f32[]{:T(128)} %constant.45.clone.1, f32[1024]{0:T(1024)S(1)} %bitcast.96), kind=kCustom, calls=%fused_computation.103 | custom fusion | flops 262144 | bytes 1060868 | tf_op jit(solution)/shard_map/scatter-add | solution.py:125
  199.0 6.7 %scatter_custom_fusion.1 = f32[1040,128]{1,0:T(8,128)S(1)} fusion(f32[1040,128]{1,0:T(8,128)S(1)} %scatter_custom_fusion, s32[1024]{0:T(1024)S(1)} %get-tuple-element.59, f32[1024,128]{1,0:T(8,128)S(1)} %convolution_multiply_fusion.2, f32[1024]{0:T(1024)S(1)} %bitcast.94), kind=kCustom, calls=%fused_computation.101 | custom fusion | flops 262144 | bytes 1060864 | tf_op jit(solution)/shard_map/scatter-add | solution.py:125
  205.7 6.7 %scatter_custom_fusion.2 = f32[1040,128]{1,0:T(8,128)S(1)} fusion(f32[1040,128]{1,0:T(8,128)S(1)} %scatter_custom_fusion.1, s32[1024]{0:T(1024)S(1)} %get-tuple-element.49, f32[1024,128]{1,0:T(8,128)S(1)} %convolution_multiply_fusion.2, f32[1024]{0:T(1024)S(1)} %bitcast.92), kind=kCustom, calls=%fused_computation.99 | custom fusion | flops 262144 | bytes 1060864 | tf_op jit(solution)/shard_map/scatter-add | solution.py:125
  212.5 7.1 %scatter_custom_fusion.3 = f32[1040,128]{1,0:T(8,128)S(1)} fusion(f32[1040,128]{1,0:T(8,128)S(1)} %scatter_custom_fusion.2, s32[1024]{0:T(1024)S(1)} %get-tuple-element.17, f32[1024,128]{1,0:T(8,128)S(1)} %convolution_multiply_fusion.2, f32[1024]{0:T(1024)S(1)} %bitcast.90), kind=kCustom, calls=%fused_computation.97 | custom fusion | flops 262144 | bytes 1060864 | tf_op jit(solution)/shard_map/scatter-add | solution.py:125
  219.8 3.5 scatter_fusion
  224.4 5.0 %collective-permute-done.9 = f32[16,33,128]{2,0,1:T(8,128)S(1)} collective-permute-done((f32[16,33,128]{2,0,1:T(8,128)S(1)}, f32[16,33,128]{2,0,1:T(8,128)S(1)}, u32[]{:S(2)}, u32[]{:S(2)}) %collective-permute-start.9) | collective-permute-done | bytes 270368 | tf_op jit(solution)/shard_map/ppermute | solution.py:33
  231.6 39.5 %all-reduce.5.cloned.1.call-done = f32[4,32,16,128]{3,1,2,0:T(8,128)} async-done(((f32[4,32,16,128]{3,1,2,0:T(8,128)}), f32[4,32,16,128]{3,1,2,0:T(8,128)}) %all-reduce.5.cloned.1.call-update) | async-done | bytes 1048592 | tf_op jit(solution)/shard_map/psum | solution.py:176
  271.1 1.8 copy.65
  272.9 3.4 fusion.1
  277.2 1.5 collective-permute-start.10
  278.7 2.3 collective-permute-start.11
  281.2 12.7 %collective-permute-done.10 = f32[8,32,4,128]{3,1,2,0:T(8,128)S(1)} collective-permute-done((f32[8,32,4,128]{3,1,2,0:T(8,128)S(1)}, f32[8,32,4,128]{3,1,2,0:T(8,128)S(1)}, u32[]{:S(2)}, u32[]{:S(2)}) %collective-permute-start.10) | collective-permute-done | bytes 524320 | tf_op jit(solution)/shard_map/ppermute | solution.py:21
  293.9 9.3 %collective-permute-done.11 = f32[8,32,4,128]{3,1,2,0:T(8,128)S(1)} collective-permute-done((f32[8,32,4,128]{3,1,2,0:T(8,128)S(1)}, f32[8,32,4,128]{3,1,2,0:T(8,128)S(1)}, u32[]{:S(2)}, u32[]{:S(2)}) %collective-permute-start.11) | collective-permute-done | bytes 524320 | tf_op jit(solution)/shard_map/ppermute | solution.py:23
  303.5 3.7 fusion.87
  307.2 3.4 copy.67
  310.6 3.4 copy.68
  314.5 2.9 fusion.34
  317.3 1.6 copy.79
  318.9 6.8 %collective-permute-done.12 = f32[8,32,24,4]{1,2,3,0:T(8,128)} collective-permute-done((f32[8,32,24,4]{1,2,3,0:T(8,128)}, f32[8,32,24,4]{1,2,3,0:T(8,128)}, u32[]{:S(2)}, u32[]{:S(2)}) %collective-permute-start.12) | collective-permute-done | bytes 98336 | tf_op jit(solution)/shard_map/ppermute | solution.py:21
  325.7 3.6 copy.69
  329.3 3.4 copy.70
  332.7 5.7 %pad_maximum_fusion.1 = f32[8,32,24,136]{3,1,2,0:T(8,128)S(1)} fusion(f32[8,32,24,4]{3,1,2,0:T(8,128)} %copy.70, f32[8,32,4,128]{3,1,2,0:T(8,128)S(1)} %collective-permute-done.11, f32[8,32,16,128]{3,1,2,0:T(8,128)S(1)} %copy_multiply_fusion, f32[8,32,4,128]{3,1,2,0:T(8,128)S(1)} %collective-permute-done.10, f32[8,32,24,4]{3,1,2,0:T(8,128)} %copy.69), kind=kLoop, calls=%fused_computation.17 | loop fusion | flops 3342336 | bytes 6684672 | tf_op jit(solution)/shard_map/concatenate | solution.py:19
  339.8 2.8 slice.405
  342.6 2.3 rev.25
  344.9 2.3 rev.24
  347.2 6.6 %maximum_select_fusion.2 = f32[8,32,24,136]{3,1,2,0:T(8,128)S(1)} fusion(f32[8,32,20,136]{3,1,2,0:T(8,128)} %slice.405, f32[8,32,4,136]{3,1,2,0:T(8,128)} %rev.24, pred[]{:T(512)S(6)} %eq.20, f32[8,32,24,4]{3,1,2,0:T(8,128)} %copy.70, f32[8,32,4,128]{3,1,2,0:T(8,128)S(1)} %collective-permute-done.11, f32[8,32,16,128]{3,1,2,0:T(8,128)S(1)} %copy_multiply_fusion, ...), kind=kLoop, calls=%fused_computation.18 | loop fusion | flops 5013504 | bytes 10027009 | tf_op jit(solution)/shard_map/jit(_where)/select_n | solution.py:50
  355.1 3.6 broadcast_multiply_fusion
  358.7 12.1 %broadcast_multiply_fusion.1 = (f32[8,32,22,134]{3,1,2,0:T(8,128)}, f32[8,32,22,134]{3,1,2,0:T(8,128)}) fusion(f32[22,134]{1,0:T(8,128)S(1)} %slice_bitcast_fusion.2, f32[8,32,24,136]{3,1,2,0:T(8,128)S(1)} %get-tuple-element.15, f32[8,32,24,136]{3,1,2,0:T(8,128)} %get-tuple-element.16), kind=kLoop, calls=%fused_computation.59 | loop fusion | flops 5282816 | bytes 24161808 | tf_op jit(solution)/shard_map/mul | solution.py:76
  370.7 14.0 %broadcast_multiply_fusion.2 = (f32[8,32,20,132]{3,1,2,0:T(8,128)S(1)}, f32[8,32,20,132]{3,1,2,0:T(8,128)S(1)}) fusion(f32[20,132]{1,0:T(8,128)S(1)} %slice_bitcast_fusion.1, f32[8,32,22,134]{3,1,2,0:T(8,128)} %get-tuple-element.13, f32[8,32,22,134]{3,1,2,0:T(8,128)} %get-tuple-element.14), kind=kLoop, calls=%fused_computation.60 | loop fusion | flops 4730880 | bytes 21637440 | tf_op jit(solution)/shard_map/mul | solution.py:76
  384.8 7.6 %broadcast_multiply_fusion.3 = (f32[8,32,18,130]{3,1,2,0:T(8,128)S(1)}, f32[8,32,18,130]{3,1,2,0:T(8,128)}) fusion(f32[18,130]{1,0:T(8,128)S(1)} %slice_bitcast_fusion, f32[8,32,20,132]{3,1,2,0:T(8,128)S(1)} %get-tuple-element.11, f32[8,32,20,132]{3,1,2,0:T(8,128)S(1)} %get-tuple-element.12), kind=kLoop, calls=%fused_computation.61 | loop fusion | flops 4193280 | bytes 19178640 | tf_op jit(solution)/shard_map/mul | solution.py:76
  392.5 6.8 %bitcast_add_fusion = f32[8,32,16,128]{3,1,2,0:T(8,128)S(1)} fusion(f32[8,32,16,128]{3,2,1,0:T(8,128)S(1)} %copy-done.4, f32[8,32,18,130]{3,1,2,0:T(8,128)S(1)} %get-tuple-element.9, f32[8,32,18,130]{3,1,2,0:T(8,128)} %get-tuple-element.10, s32[32]{0:T(128)S(1)} %copy-done.17, s32[32]{0:T(128)S(1)} %copy-done.15), kind=kOutput, calls=%fused_computation.77 | convolution fusion | flops 205005824 | bytes 16778240 | tf_op jit(solution)/shard_map/lm,klyx->kmyx/dot_general | solution.py:183
  399.3 2.5 copy.78
  (117 shorter events, 25.9 us)
Async XLA Ops:
  7.2 161.2 %copy-start = (f32[4,32,32]{2,1,0:T(8,128)S(1)}, f32[4,32,32]{2,1,0:T(8,128)}, u32[]{:S(2)}) copy-start(f32[4,32,32]{2,1,0:T(8,128)} %param.21) | copy-start | bytes 49156
  7.2 16.1 %copy-start.9 = (f32[16,128]{1,0:T(8,128)S(1)}, f32[16,128]{1,0:T(8,128)}, u32[]{:S(2)}) copy-start(f32[16,128]{1,0:T(8,128)} %param.19) | copy-start | bytes 24580
  7.2 15.4 %copy-start.19 = (s32[1,2]{1,0:T(1,128)S(1)}, s32[1,2]{1,0:T(1,128)}, u32[]{:S(2)}) copy-start(s32[1,2]{1,0:T(1,128)} %param.22) | copy-start | bytes 28
  7.2 161.1 %all-reduce.3.cloned.1.call-start = ((), (), s32[]{:S(2)}) async-start(), calls=%async_computation | async-start | bytes 2097152 | tf_op jit(solution)/shard_map/psum | solution.py:165
  8.0 15.3 %collective-permute-start.4 = (f32[1,1,4,128]{3,2,1,0:T(4,128)S(1)}, f32[1,1,4,128]{3,2,1,0:T(4,128)S(1)}, u32[]{:S(2)}, u32[]{:S(2)}) collective-permute-start(f32[1,1,4,128]{3,2,1,0:T(4,128)S(1)} %get-tuple-element.47), channel_id=1, source_target_pairs={{0,4},{4,8},{8,12},{12,0},{1,5},{5,9},{9,13},{13,1},{2,6},{6,10},{... | collective-permute-start | bytes 6152 | tf_op jit(solution)/shard_map/ppermute | solution.py:21
  11.0 12.3 %collective-permute-start.5 = (f32[1,1,4,128]{3,2,1,0:T(4,128)S(1)}, f32[1,1,4,128]{3,2,1,0:T(4,128)S(1)}, u32[]{:S(2)}, u32[]{:S(2)}) collective-permute-start(f32[1,1,4,128]{3,2,1,0:T(4,128)S(1)} %get-tuple-element.48), channel_id=1, source_target_pairs={{4,0},{8,4},{12,8},{0,12},{5,1},{9,5},{13,9},{1,13},{6,2},{10,6},{... | collective-permute-start | bytes 6152 | tf_op jit(solution)/shard_map/ppermute | solution.py:23
  13.8 12.8 %copy-start.14 = (s32[32]{0:T(128)}, s32[32]{0:T(128)S(1)}, u32[]{:S(2)}) copy-start(s32[32]{0:T(128)S(1)} %get-tuple-element.61) | copy-start | bytes 388
  13.8 12.8 %copy-start.16 = (s32[32]{0:T(128)}, s32[32]{0:T(128)S(1)}, u32[]{:S(2)}) copy-start(s32[32]{0:T(128)S(1)} %get-tuple-element.62) | copy-start | bytes 388
  18.7 16.8 %collective-permute-start = (f32[8,32,4,128]{3,1,2,0:T(8,128)}, f32[8,32,4,128]{3,1,2,0:T(8,128)S(1)}, u32[]{:S(2)}, u32[]{:S(2)}) collective-permute-start(f32[8,32,4,128]{3,1,2,0:T(8,128)} %get-tuple-element.31), channel_id=1, source_target_pairs={{0,4},{4,8},{8,12},{12,0},{1,5},{5,9},{9,13},{13,1},{2,6},{6,10},{... | collective-permute-start | bytes 1572872 | tf_op jit(solution)/shard_map/ppermute | solution.py:21
  18.7 24.8 %collective-permute-start.1 = (f32[8,32,4,128]{3,1,2,0:T(8,128)}, f32[8,32,4,128]{3,1,2,0:T(8,128)S(1)}, u32[]{:S(2)}, u32[]{:S(2)}) collective-permute-start(f32[8,32,4,128]{3,1,2,0:T(8,128)} %get-tuple-element.32), channel_id=1, source_target_pairs={{4,0},{8,4},{12,8},{0,12},{5,1},{9,5},{13,9},{1,13},{6,2},{10,6},{... | collective-permute-start | bytes 1572872 | tf_op jit(solution)/shard_map/ppermute | solution.py:23
  23.4 3.1 collective-permute-start.6
  23.4 3.1 collective-permute-start.7
  54.3 15.2 %collective-permute-start.3 = (f32[8,32,24,4]{1,2,3,0:T(8,128)}, f32[8,32,24,4]{1,2,3,0:T(8,128)}, u32[]{:S(2)}, u32[]{:S(2)}) collective-permute-start(f32[8,32,24,4]{1,2,3,0:T(8,128)} %copy.53), channel_id=1, source_target_pairs={{1,0},{2,1},{3,2},{0,3},{5,4},{6,5},{7,6},{4,7},{9,8},{10,9},{11,1... | collective-permute-start | bytes 294920 | tf_op jit(solution)/shard_map/ppermute | solution.py:23
  54.4 11.8 %collective-permute-start.2 = (f32[8,32,24,4]{1,2,3,0:T(8,128)}, f32[8,32,24,4]{1,2,3,0:T(8,128)}, u32[]{:S(2)}, u32[]{:S(2)}) collective-permute-start(f32[8,32,24,4]{1,2,3,0:T(8,128)} %copy.52), channel_id=1, source_target_pairs={{0,1},{1,2},{2,3},{3,0},{4,5},{5,6},{6,7},{7,4},{8,9},{9,10},{10,1... | collective-permute-start | bytes 294920 | tf_op jit(solution)/shard_map/ppermute | solution.py:21
  94.1 2.6 copy-start.2
  96.8 2.8 copy-start.7
  124.6 2.2 copy-start.3
  126.8 2.9 copy-start.18
  126.8 3.0 copy-start.13
  126.8 41.5 %copy-start.6 = (f32[4,32,16,128]{3,2,1,0:T(8,128)S(1)}, f32[4,32,16,128]{3,2,1,0:T(8,128)}, u32[]{:S(2)}) copy-start(f32[4,32,16,128]{3,2,1,0:T(8,128)} %param.18) | copy-start | bytes 3145732
  129.0 142.1 %all-reduce.5.cloned.1.call-start = ((), (), s32[]{:S(2)}) async-start(), calls=%async_computation.1 | async-start | bytes 2097152 | tf_op jit(solution)/shard_map/psum | solution.py:176
  171.8 3.6 collective-permute-start.8
  176.2 13.2 %copy-start.8 = (bf16[1024,128]{1,0:T(8,128)(2,1)S(1)}, bf16[1024,128]{1,0:T(8,128)(2,1)}, u32[]{:S(2)}) copy-start(bf16[1024,128]{1,0:T(8,128)(2,1)} %param.25) | copy-start | bytes 786436
  176.5 14.3 %copy-start.10 = (f32[8,1024]{1,0:T(8,128)S(1)}, f32[8,1024]{1,0:T(8,128)}, u32[]{:S(2)}) copy-start(f32[8,1024]{1,0:T(8,128)} %param.27) | copy-start | bytes 98308
  176.5 14.3 %copy-start.11 = (f32[8,1024]{1,0:T(8,128)S(1)}, f32[8,1024]{1,0:T(8,128)}, u32[]{:S(2)}) copy-start(f32[8,1024]{1,0:T(8,128)} %param.26) | copy-start | bytes 98308
  176.5 14.3 %copy-start.12 = (f32[8,128]{1,0:T(8,128)S(1)}, f32[8,128]{1,0:T(8,128)}, u32[]{:S(2)}) copy-start(f32[8,128]{1,0:T(8,128)} %param.28) | copy-start | bytes 12292
  223.4 6.1 %collective-permute-start.9 = (f32[16,33,128]{2,0,1:T(8,128)S(1)}, f32[16,33,128]{2,0,1:T(8,128)S(1)}, u32[]{:S(2)}, u32[]{:S(2)}) collective-permute-start(f32[16,33,128]{2,0,1:T(8,128)S(1)} %slice.398), channel_id=1, source_target_pairs={{0,1},{1,2},{2,3},{3,0},{4,5},{5,6},{6,7},{7,4},{8,9},{9,10},{10,1... | collective-permute-start | bytes 811016 | tf_op jit(solution)/shard_map/ppermute | solution.py:33
  277.2 16.7 %collective-permute-start.10 = (f32[8,32,4,128]{3,1,2,0:T(8,128)S(1)}, f32[8,32,4,128]{3,1,2,0:T(8,128)S(1)}, u32[]{:S(2)}, u32[]{:S(2)}) collective-permute-start(f32[8,32,4,128]{3,1,2,0:T(8,128)S(1)} %get-tuple-element.29), channel_id=1, source_target_pairs={{0,4},{4,8},{8,12},{12,0},{1,5},{5,9},{9,13},{13,1},{2,6},{6,10},{... | collective-permute-start | bytes 1572872 | tf_op jit(solution)/shard_map/ppermute | solution.py:21
  278.7 24.5 %collective-permute-start.11 = (f32[8,32,4,128]{3,1,2,0:T(8,128)S(1)}, f32[8,32,4,128]{3,1,2,0:T(8,128)S(1)}, u32[]{:S(2)}, u32[]{:S(2)}) collective-permute-start(f32[8,32,4,128]{3,1,2,0:T(8,128)S(1)} %get-tuple-element.30), channel_id=1, source_target_pairs={{4,0},{8,4},{12,8},{0,12},{5,1},{9,5},{13,9},{1,13},{6,2},{10,6},{... | collective-permute-start | bytes 1572872 | tf_op jit(solution)/shard_map/ppermute | solution.py:23
  314.0 15.4 %collective-permute-start.13 = (f32[8,32,24,4]{1,2,3,0:T(8,128)}, f32[8,32,24,4]{1,2,3,0:T(8,128)}, u32[]{:S(2)}, u32[]{:S(2)}) collective-permute-start(f32[8,32,24,4]{1,2,3,0:T(8,128)} %copy.68), channel_id=1, source_target_pairs={{1,0},{2,1},{3,2},{0,3},{5,4},{6,5},{7,6},{4,7},{9,8},{10,9},{11,1... | collective-permute-start | bytes 294920 | tf_op jit(solution)/shard_map/ppermute | solution.py:23
  314.5 11.3 %collective-permute-start.12 = (f32[8,32,24,4]{1,2,3,0:T(8,128)}, f32[8,32,24,4]{1,2,3,0:T(8,128)}, u32[]{:S(2)}, u32[]{:S(2)}) collective-permute-start(f32[8,32,24,4]{1,2,3,0:T(8,128)} %copy.67), channel_id=1, source_target_pairs={{0,1},{1,2},{2,3},{3,0},{4,5},{5,6},{6,7},{7,4},{8,9},{9,10},{10,1... | collective-permute-start | bytes 294920 | tf_op jit(solution)/shard_map/ppermute | solution.py:21
  353.9 1.2 copy-start.5
  384.8 7.7 %copy-start.4 = (f32[8,32,16,128]{3,2,1,0:T(8,128)S(1)}, f32[8,32,16,128]{3,2,1,0:T(8,128)}, u32[]{:S(2)}) copy-start(f32[8,32,16,128]{3,2,1,0:T(8,128)} %param.16) | copy-start | bytes 6291460
  384.8 7.7 %copy-start.15 = (s32[32]{0:T(128)S(1)}, s32[32]{0:T(128)}, u32[]{:S(2)}) copy-start(s32[32]{0:T(128)} %copy-done.14) | copy-start | bytes 388
  384.8 7.7 %copy-start.17 = (s32[32]{0:T(128)S(1)}, s32[32]{0:T(128)}, u32[]{:S(2)}) copy-start(s32[32]{0:T(128)} %copy-done.16) | copy-start | bytes 388
  392.5 9.3 %copy-start.1 = (f32[4,32,32]{2,1,0:T(8,128)S(1)}, f32[4,32,32]{2,1,0:T(8,128)}, u32[]{:S(2)}) copy-start(f32[4,32,32]{2,1,0:T(8,128)} %param.21) | copy-start | bytes 49156
Sparse Core Ops, SparseCore 0:
  129.1 39.1 all-reduce.2
  231.7 39.3 all-reduce.4
where the time goes:
time: 414 us; the launch traced here: 409 us
  waiting for transfers between devices  142 us (34%)
  other arithmetic  126 us (30%)
  local copies, waits for them, and re-layouts  88.7 us (21%)
  starting transfers between devices  18.1 us (4%)
  matrix products  17.5 us (4%)
  between operations  16.3 us (4%)
    psum x1, waiting for transfers between devices, body(): gradient_cells = lax.psum(tile_grad, 'mem')  39.5 us
    ppermute x6, waiting for transfers between devices, padded_2(): lax.ppermute(tail, axis, [(i, (i + 1) % count) for i in range(count)])  39.3 us
    psum x1, waiting for transfers between devices, body(): member_total = lax.psum(partial_sum, 'mem')  38.5 us
    mul x4, other arithmetic, sweep_adjoint(): stencil_sum = stencil_of(kappa_pad * padded)  37.3 us
    scatter-add x4, other arithmetic, observe(): returned.at[cell_index[corner]]  27.2 us
    add x4, other arithmetic, sweep_forward(): padded = padded[:, :, 1:-1, 1:-1] + kappa_pad * stencil_sum  19.1 us
    ppermute x6, waiting for transfers between devices, padded_2(): lax.ppermute(head, axis, [((i + 1) % count, i) for i in range(count)])  17.4 us
    slice x8, local copies, waits for them, and re-layouts, padded_2(): lax.slice_in_dim(cells, cells.shape[dim] - width, cells.shape[dim], axis=...  16.1 us
  transfers between devices with their start and end apart: 16, of which 11 were waited for; matrix products, arithmetic and copies ran while one was open for 5% of the time, Pallas kernels for 0%

commit v1 on v0

--- a/solution.py
+++ b/solution.py
@@ -162,7 +162,7 @@
     kappa_pad = deep_pad(kappa[None, None], NDIFF)
     spread = sweep_forward(deep_pad(spread, NDIFF), kappa_pad)
     partial_sum = jnp.sum(perturb.astype(jnp.float32) * spread[:, None], axis=0)
-    member_total = lax.psum(partial_sum, "mem")
+    member_total = jnp.sum(lax.all_gather(partial_sum, "mem"), axis=0)
     static = jnp.einsum("vlm,vmyx->vlyx", static_vert, chi, precision=highest)
     increment = (ens_scale * member_total + static_weight * static).astype(jnp.bfloat16)
     widened = extend_east(to_cells(increment, column_width), rim_cols)

time: 414 us -> 407 us (0.983)
  waiting for transfers between devices: 142 us -> 135 us
    psum x1 -> x0, waiting for transfers between devices: 38.5 us -> none  [body(): member_total = lax.psum(partial_sum, 'mem')]
    all_gather x0 -> x1, waiting for transfers between devices: none -> 29.7 us  [body(): member_total = jnp.sum(lax.all_gather(partial_sum, 'mem'), axis=0)]
where the time goes in v1:
time: 407 us; the launch traced here: 402 us
  waiting for transfers between devices  135 us (33%)
  other arithmetic  129 us (32%)
  local copies, waits for them, and re-layouts  87.3 us (21%)
  starting transfers between devices  18.3 us (4%)
  matrix products  16.6 us (4%)
  between operations  16.5 us (4%)
    ppermute x6, waiting for transfers between devices, padded_2(): lax.ppermute(tail, axis, [(i, (i + 1) % count) for i in range(count)])  40.8 us
    psum x1, waiting for transfers between devices, body(): gradient_cells = lax.psum(tile_grad, 'mem')  39.5 us
    mul x4, other arithmetic, sweep_adjoint(): stencil_sum = stencil_of(kappa_pad * padded)  37.3 us
    all_gather x1, waiting for transfers between devices, body(): member_total = jnp.sum(lax.all_gather(partial_sum, 'mem'), axis=0)  29.7 us
    scatter-add x4, other arithmetic, observe(): returned.at[cell_index[corner]]  27 us
    add x4, other arithmetic, sweep_forward(): padded = padded[:, :, 1:-1, 1:-1] + kappa_pad * stencil_sum  19.2 us
    ppermute x6, waiting for transfers between devices, padded_2(): lax.ppermute(head, axis, [((i + 1) % count, i) for i in range(count)])  17.4 us
    slice x8, local copies, waits for them, and re-layouts, padded_2(): lax.slice_in_dim(cells, cells.shape[dim] - width, cells.shape[dim], axis=...  16.1 us
  transfers between devices with their start and end apart: 16, of which 11 were waited for; matrix products, arithmetic and copies ran while one was open for 5% of the time, Pallas kernels for 0%

profile of v1, /device:TPU:0, one launch (start us, length us, event | category | flops | bytes accessed | tf_op | source)
XLA Modules:
  0.0 402.2 jit_solution(10909949520491467498)
XLA Ops:
  7.9 3.1 collective-permute-start.4
  11.0 2.0 collective-permute-start.5
  13.8 3.9 fusion.28
  18.7 3.8 collective-permute-start.1
  22.6 1.7 collective-permute-start.7
  26.5 9.1 %collective-permute-done = f32[8,32,4,128]{3,1,2,0:T(8,128)S(1)} collective-permute-done((f32[8,32,4,128]{3,1,2,0:T(8,128)}, f32[8,32,4,128]{3,1,2,0:T(8,128)S(1)}, u32[]{:S(2)}, u32[]{:S(2)}) %collective-permute-start) | collective-permute-done | bytes 524320 | tf_op jit(solution)/shard_map/ppermute | solution.py:21
  35.5 8.0 %collective-permute-done.1 = f32[8,32,4,128]{3,1,2,0:T(8,128)S(1)} collective-permute-done((f32[8,32,4,128]{3,1,2,0:T(8,128)}, f32[8,32,4,128]{3,1,2,0:T(8,128)S(1)}, u32[]{:S(2)}, u32[]{:S(2)}) %collective-permute-start.1) | collective-permute-done | bytes 524320 | tf_op jit(solution)/shard_map/ppermute | solution.py:23
  43.9 3.7 fusion.88
  47.6 3.4 copy.81
  51.0 3.4 copy.82
  55.1 11.0 %collective-permute-done.2 = f32[8,32,24,4]{1,2,3,0:T(8,128)} collective-permute-done((f32[8,32,24,4]{1,2,3,0:T(8,128)}, f32[8,32,24,4]{1,2,3,0:T(8,128)}, u32[]{:S(2)}, u32[]{:S(2)}) %collective-permute-start.2) | collective-permute-done | bytes 98336 | tf_op jit(solution)/shard_map/ppermute | solution.py:21
  66.1 3.4 copy.83
  69.6 3.4 copy.84
  72.9 5.7 %pad_maximum_fusion = f32[8,32,24,136]{3,1,2,0:T(8,128)S(1)} fusion(f32[8,32,24,4]{3,1,2,0:T(8,128)} %copy.84, f32[8,32,4,128]{3,1,2,0:T(8,128)S(1)} %collective-permute-done.1, f32[8,32,16,128]{3,1,2,0:T(8,128)S(1)} %fusion.28, f32[8,32,4,128]{3,1,2,0:T(8,128)S(1)} %collective-permute-done, f32[8,32,24,4]{3,1,2,0:T(8,128)} %copy.83), kind=kLoop, calls=%fused_computation.14 | loop fusion | flops 3342336 | bytes 6684672 | tf_op jit(solution)/shard_map/concatenate | solution.py:19
  80.1 2.8 slice.361
  82.8 2.3 rev.21
  85.2 2.3 rev.20
  87.5 6.6 %maximum_select_fusion = f32[8,32,24,136]{3,1,2,0:T(8,128)S(1)} fusion(f32[8,32,20,136]{3,1,2,0:T(8,128)} %slice.361, f32[8,32,4,136]{3,1,2,0:T(8,128)} %rev.20, pred[]{:T(512)S(6)} %eq.20, f32[8,32,24,4]{3,1,2,0:T(8,128)} %copy.84, f32[8,32,4,128]{3,1,2,0:T(8,128)S(1)} %collective-permute-done.1, f32[8,32,16,128]{3,1,2,0:T(8,128)S(1)} %fusion.28, ...), kind=kLoop, calls=%fused_computation.15 | loop fusion | flops 5013504 | bytes 10027009 | tf_op jit(solution)/shard_map/jit(_where)/select_n | solution.py:50
  94.1 2.6 copy-done.2
  96.8 2.8 slice.362
  99.6 5.9 %maximum_select_fusion.1 = f32[8,32,24,136]{3,1,2,0:T(8,128)S(1)} fusion(f32[8,32,24,136]{3,1,2,0:T(8,128)} %copy-done.2, f32[8,32,4,136]{3,1,2,0:T(8,128)S(1)} %copy-done.7, f32[8,32,20,136]{3,1,2,0:T(8,128)} %slice.362, pred[]{:T(512)S(6)} %eq.19), kind=kLoop, calls=%fused_computation.16 | loop fusion | flops 1671168 | bytes 10027009 | tf_op jit(solution)/shard_map/jit(_where)/select_n | solution.py:52
  105.5 6.1 %fusion.6 = f32[8,32,22,134]{3,1,2,0:T(8,128)S(1)} fusion(f32[8,32,24,136]{3,1,2,0:T(8,128)S(1)} %maximum_select_fusion.1, f32[22,134]{1,0:T(8,128)S(1)} %slice_bitcast_fusion.2), kind=kLoop, calls=%fused_computation.29 | loop fusion | flops 5282816 | bytes 18124304 | tf_op jit(solution)/shard_map/add | solution.py:70
  111.6 5.8 %fusion.11 = f32[8,32,20,132]{3,1,2,0:T(8,128)S(1)} fusion(f32[8,32,22,134]{3,1,2,0:T(8,128)S(1)} %fusion.6, f32[20,132]{1,0:T(8,128)S(1)} %slice_bitcast_fusion.1), kind=kLoop, calls=%fused_computation.41 | loop fusion | flops 4730880 | bytes 16230720 | tf_op jit(solution)/shard_map/add | solution.py:70
  117.4 5.0 %fusion.16 = f32[8,32,18,130]{3,1,2,0:T(8,128)S(1)} fusion(f32[8,32,20,132]{3,1,2,0:T(8,128)S(1)} %fusion.11, f32[18,130]{1,0:T(8,128)S(1)} %slice_bitcast_fusion), kind=kLoop, calls=%fused_computation.53 | loop fusion | flops 4193280 | bytes 14386320 | tf_op jit(solution)/shard_map/add | solution.py:70
  122.5 2.2 fusion.25
  126.9 1.8 fusion
  131.3 29.7 %all-gather.3.cloned.1.call-done = f32[8,32,16,128]{3,2,1,0:T(8,128)} async-done(((f32[4,32,16,128]{3,2,1,0:T(8,128)}), f32[8,32,16,128]{3,2,1,0:T(8,128)}) %all-gather.3.cloned.1.call-update) | async-done | bytes 2097168 | tf_op jit(solution)/shard_map/all_gather | solution.py:165
  161.1 1.9 reduce_sum.38
  166.4 2.4 collective-permute-done.8
  170.0 3.2 gather_fusion.4
  173.2 3.2 gather_fusion.3
  176.5 3.2 gather_fusion.2
  179.7 3.2 gather_fusion.1
  185.9 6.7 %scatter_custom_fusion = f32[1040,128]{1,0:T(8,128)S(1)} fusion(s32[1024]{0:T(1024)S(1)} %get-tuple-element.66, f32[1024,128]{1,0:T(8,128)S(1)} %convolution_multiply_fusion.2, f32[]{:T(128)} %constant.45.clone.1, f32[1024]{0:T(1024)S(1)} %bitcast.98), kind=kCustom, calls=%fused_computation.104 | custom fusion | flops 262144 | bytes 1060868 | tf_op jit(solution)/shard_map/scatter-add | solution.py:125
  192.5 6.7 %scatter_custom_fusion.1 = f32[1040,128]{1,0:T(8,128)S(1)} fusion(f32[1040,128]{1,0:T(8,128)S(1)} %scatter_custom_fusion, s32[1024]{0:T(1024)S(1)} %get-tuple-element.61, f32[1024,128]{1,0:T(8,128)S(1)} %convolution_multiply_fusion.2, f32[1024]{0:T(1024)S(1)} %bitcast.96), kind=kCustom, calls=%fused_computation.102 | custom fusion | flops 262144 | bytes 1060864 | tf_op jit(solution)/shard_map/scatter-add | solution.py:125
  199.2 6.9 %scatter_custom_fusion.2 = f32[1040,128]{1,0:T(8,128)S(1)} fusion(f32[1040,128]{1,0:T(8,128)S(1)} %scatter_custom_fusion.1, s32[1024]{0:T(1024)S(1)} %get-tuple-element.51, f32[1024,128]{1,0:T(8,128)S(1)} %convolution_multiply_fusion.2, f32[1024]{0:T(1024)S(1)} %bitcast.94), kind=kCustom, calls=%fused_computation.100 | custom fusion | flops 262144 | bytes 1060864 | tf_op jit(solution)/shard_map/scatter-add | solution.py:125
  206.1 6.7 %scatter_custom_fusion.3 = f32[1040,128]{1,0:T(8,128)S(1)} fusion(f32[1040,128]{1,0:T(8,128)S(1)} %scatter_custom_fusion.2, s32[1024]{0:T(1024)S(1)} %get-tuple-element.19, f32[1024,128]{1,0:T(8,128)S(1)} %convolution_multiply_fusion.2, f32[1024]{0:T(1024)S(1)} %bitcast.92), kind=kCustom, calls=%fused_computation.98 | custom fusion | flops 262144 | bytes 1060864 | tf_op jit(solution)/shard_map/scatter-add | solution.py:125
  213.1 3.5 scatter_fusion
  217.7 5.0 %collective-permute-done.9 = f32[16,33,128]{2,0,1:T(8,128)S(1)} collective-permute-done((f32[16,33,128]{2,0,1:T(8,128)S(1)}, f32[16,33,128]{2,0,1:T(8,128)S(1)}, u32[]{:S(2)}, u32[]{:S(2)}) %collective-permute-start.9) | collective-permute-done | bytes 270368 | tf_op jit(solution)/shard_map/ppermute | solution.py:33
  224.8 39.5 %all-reduce.2.cloned.1.call-done = f32[4,32,16,128]{3,1,2,0:T(8,128)} async-done(((f32[4,32,16,128]{3,1,2,0:T(8,128)}), f32[4,32,16,128]{3,1,2,0:T(8,128)}) %all-reduce.2.cloned.1.call-update) | async-done | bytes 1048592 | tf_op jit(solution)/shard_map/psum | solution.py:176
  264.3 1.8 copy.94
  266.2 3.4 fusion.1
  272.0 2.3 collective-permute-start.11
  274.4 12.7 %collective-permute-done.10 = f32[8,32,4,128]{3,1,2,0:T(8,128)S(1)} collective-permute-done((f32[8,32,4,128]{3,1,2,0:T(8,128)S(1)}, f32[8,32,4,128]{3,1,2,0:T(8,128)S(1)}, u32[]{:S(2)}, u32[]{:S(2)}) %collective-permute-start.10) | collective-permute-done | bytes 524320 | tf_op jit(solution)/shard_map/ppermute | solution.py:21
  287.1 9.3 %collective-permute-done.11 = f32[8,32,4,128]{3,1,2,0:T(8,128)S(1)} collective-permute-done((f32[8,32,4,128]{3,1,2,0:T(8,128)S(1)}, f32[8,32,4,128]{3,1,2,0:T(8,128)S(1)}, u32[]{:S(2)}, u32[]{:S(2)}) %collective-permute-start.11) | collective-permute-done | bytes 524320 | tf_op jit(solution)/shard_map/ppermute | solution.py:23
  296.8 3.7 fusion.87
  300.5 3.4 copy.96
  303.8 3.4 copy.97
  307.9 2.9 fusion.34
  310.8 1.6 copy.108
  312.4 6.6 %collective-permute-done.12 = f32[8,32,24,4]{1,2,3,0:T(8,128)} collective-permute-done((f32[8,32,24,4]{1,2,3,0:T(8,128)}, f32[8,32,24,4]{1,2,3,0:T(8,128)}, u32[]{:S(2)}, u32[]{:S(2)}) %collective-permute-start.12) | collective-permute-done | bytes 98336 | tf_op jit(solution)/shard_map/ppermute | solution.py:21
  319.0 3.4 copy.98
  322.4 3.4 copy.99
  325.8 5.7 %pad_maximum_fusion.1 = f32[8,32,24,136]{3,1,2,0:T(8,128)S(1)} fusion(f32[8,32,24,4]{3,1,2,0:T(8,128)} %copy.99, f32[8,32,4,128]{3,1,2,0:T(8,128)S(1)} %collective-permute-done.11, f32[8,32,16,128]{3,1,2,0:T(8,128)S(1)} %copy_multiply_fusion, f32[8,32,4,128]{3,1,2,0:T(8,128)S(1)} %collective-permute-done.10, f32[8,32,24,4]{3,1,2,0:T(8,128)} %copy.98), kind=kLoop, calls=%fused_computation.17 | loop fusion | flops 3342336 | bytes 6684672 | tf_op jit(solution)/shard_map/concatenate | solution.py:19
  333.0 2.8 slice.405
  335.7 2.3 rev.25
  338.1 2.3 rev.24
  340.4 6.6 %maximum_select_fusion.2 = f32[8,32,24,136]{3,1,2,0:T(8,128)S(1)} fusion(f32[8,32,20,136]{3,1,2,0:T(8,128)} %slice.405, f32[8,32,4,136]{3,1,2,0:T(8,128)} %rev.24, pred[]{:T(512)S(6)} %eq.20, f32[8,32,24,4]{3,1,2,0:T(8,128)} %copy.99, f32[8,32,4,128]{3,1,2,0:T(8,128)S(1)} %collective-permute-done.11, f32[8,32,16,128]{3,1,2,0:T(8,128)S(1)} %copy_multiply_fusion, ...), kind=kLoop, calls=%fused_computation.18 | loop fusion | flops 5013504 | bytes 10027009 | tf_op jit(solution)/shard_map/jit(_where)/select_n | solution.py:50
  348.2 3.6 broadcast_multiply_fusion
  351.8 12.1 %broadcast_multiply_fusion.1 = (f32[8,32,22,134]{3,1,2,0:T(8,128)}, f32[8,32,22,134]{3,1,2,0:T(8,128)}) fusion(f32[22,134]{1,0:T(8,128)S(1)} %slice_bitcast_fusion.2, f32[8,32,24,136]{3,1,2,0:T(8,128)S(1)} %get-tuple-element.17, f32[8,32,24,136]{3,1,2,0:T(8,128)} %get-tuple-element.18), kind=kLoop, calls=%fused_computation.59 | loop fusion | flops 5282816 | bytes 24161808 | tf_op jit(solution)/shard_map/mul | solution.py:76
  363.9 14.1 %broadcast_multiply_fusion.2 = (f32[8,32,20,132]{3,1,2,0:T(8,128)S(1)}, f32[8,32,20,132]{3,1,2,0:T(8,128)S(1)}) fusion(f32[20,132]{1,0:T(8,128)S(1)} %slice_bitcast_fusion.1, f32[8,32,22,134]{3,1,2,0:T(8,128)} %get-tuple-element.15, f32[8,32,22,134]{3,1,2,0:T(8,128)} %get-tuple-element.16), kind=kLoop, calls=%fused_computation.60 | loop fusion | flops 4730880 | bytes 21637440 | tf_op jit(solution)/shard_map/mul | solution.py:76
  378.0 7.6 %broadcast_multiply_fusion.3 = (f32[8,32,18,130]{3,1,2,0:T(8,128)S(1)}, f32[8,32,18,130]{3,1,2,0:T(8,128)}) fusion(f32[18,130]{1,0:T(8,128)S(1)} %slice_bitcast_fusion, f32[8,32,20,132]{3,1,2,0:T(8,128)S(1)} %get-tuple-element.13, f32[8,32,20,132]{3,1,2,0:T(8,128)S(1)} %get-tuple-element.14), kind=kLoop, calls=%fused_computation.61 | loop fusion | flops 4193280 | bytes 19178640 | tf_op jit(solution)/shard_map/mul | solution.py:76
  385.6 6.8 %bitcast_add_fusion = f32[8,32,16,128]{3,1,2,0:T(8,128)S(1)} fusion(f32[8,32,16,128]{3,2,1,0:T(8,128)S(1)} %copy-done.4, f32[8,32,18,130]{3,1,2,0:T(8,128)S(1)} %get-tuple-element.11, f32[8,32,18,130]{3,1,2,0:T(8,128)} %get-tuple-element.12, s32[32]{0:T(128)S(1)} %copy-done.17, s32[32]{0:T(128)S(1)} %copy-done.15), kind=kOutput, calls=%fused_computation.77 | convolution fusion | flops 205005824 | bytes 16778240 | tf_op jit(solution)/shard_map/lm,klyx->kmyx/dot_general | solution.py:183
  392.4 2.5 copy.107
  (117 shorter events, 27.7 us)
Async XLA Ops:
  7.2 155.8 %copy-start = (f32[4,32,32]{2,1,0:T(8,128)S(1)}, f32[4,32,32]{2,1,0:T(8,128)}, u32[]{:S(2)}) copy-start(f32[4,32,32]{2,1,0:T(8,128)} %param.21) | copy-start | bytes 49156
  7.2 15.4 %copy-start.9 = (f32[16,128]{1,0:T(8,128)S(1)}, f32[16,128]{1,0:T(8,128)}, u32[]{:S(2)}) copy-start(f32[16,128]{1,0:T(8,128)} %param.19) | copy-start | bytes 24580
  7.2 153.9 %all-gather.3.cloned.1.call-start = ((), (), s32[]{:S(2)}) async-start(), calls=%async_computation.1 | async-start | bytes 3145728 | tf_op jit(solution)/shard_map/all_gather | solution.py:165
  7.9 14.6 %collective-permute-start.4 = (f32[1,1,4,128]{3,2,1,0:T(4,128)S(1)}, f32[1,1,4,128]{3,2,1,0:T(4,128)S(1)}, u32[]{:S(2)}, u32[]{:S(2)}) collective-permute-start(f32[1,1,4,128]{3,2,1,0:T(4,128)S(1)} %get-tuple-element.49), channel_id=1, source_target_pairs={{0,4},{4,8},{8,12},{12,0},{1,5},{5,9},{9,13},{13,1},{2,6},{6,10},{... | collective-permute-start | bytes 6152 | tf_op jit(solution)/shard_map/ppermute | solution.py:21
  11.0 11.5 %collective-permute-start.5 = (f32[1,1,4,128]{3,2,1,0:T(4,128)S(1)}, f32[1,1,4,128]{3,2,1,0:T(4,128)S(1)}, u32[]{:S(2)}, u32[]{:S(2)}) collective-permute-start(f32[1,1,4,128]{3,2,1,0:T(4,128)S(1)} %get-tuple-element.50), channel_id=1, source_target_pairs={{4,0},{8,4},{12,8},{0,12},{5,1},{9,5},{13,9},{1,13},{6,2},{10,6},{... | collective-permute-start | bytes 6152 | tf_op jit(solution)/shard_map/ppermute | solution.py:23
  13.8 12.1 %copy-start.14 = (s32[32]{0:T(128)}, s32[32]{0:T(128)S(1)}, u32[]{:S(2)}) copy-start(s32[32]{0:T(128)S(1)} %get-tuple-element.63) | copy-start | bytes 388
  13.8 12.1 %copy-start.16 = (s32[32]{0:T(128)}, s32[32]{0:T(128)S(1)}, u32[]{:S(2)}) copy-start(s32[32]{0:T(128)S(1)} %get-tuple-element.64) | copy-start | bytes 388
  18.7 16.8 %collective-permute-start = (f32[8,32,4,128]{3,1,2,0:T(8,128)}, f32[8,32,4,128]{3,1,2,0:T(8,128)S(1)}, u32[]{:S(2)}, u32[]{:S(2)}) collective-permute-start(f32[8,32,4,128]{3,1,2,0:T(8,128)} %get-tuple-element.33), channel_id=1, source_target_pairs={{0,4},{4,8},{8,12},{12,0},{1,5},{5,9},{9,13},{13,1},{2,6},{6,10},{... | collective-permute-start | bytes 1572872 | tf_op jit(solution)/shard_map/ppermute | solution.py:21
  18.7 24.8 %collective-permute-start.1 = (f32[8,32,4,128]{3,1,2,0:T(8,128)}, f32[8,32,4,128]{3,1,2,0:T(8,128)S(1)}, u32[]{:S(2)}, u32[]{:S(2)}) collective-permute-start(f32[8,32,4,128]{3,1,2,0:T(8,128)} %get-tuple-element.34), channel_id=1, source_target_pairs={{4,0},{8,4},{12,8},{0,12},{5,1},{9,5},{13,9},{1,13},{6,2},{10,6},{... | collective-permute-start | bytes 1572872 | tf_op jit(solution)/shard_map/ppermute | solution.py:23
  22.6 3.1 collective-permute-start.6
  22.6 3.1 collective-permute-start.7
  54.3 15.2 %collective-permute-start.3 = (f32[8,32,24,4]{1,2,3,0:T(8,128)}, f32[8,32,24,4]{1,2,3,0:T(8,128)}, u32[]{:S(2)}, u32[]{:S(2)}) collective-permute-start(f32[8,32,24,4]{1,2,3,0:T(8,128)} %copy.82), channel_id=1, source_target_pairs={{1,0},{2,1},{3,2},{0,3},{5,4},{6,5},{7,6},{4,7},{9,8},{10,9},{11,1... | collective-permute-start | bytes 294920 | tf_op jit(solution)/shard_map/ppermute | solution.py:23
  54.3 11.8 %collective-permute-start.2 = (f32[8,32,24,4]{1,2,3,0:T(8,128)}, f32[8,32,24,4]{1,2,3,0:T(8,128)}, u32[]{:S(2)}, u32[]{:S(2)}) collective-permute-start(f32[8,32,24,4]{1,2,3,0:T(8,128)} %copy.81), channel_id=1, source_target_pairs={{0,1},{1,2},{2,3},{3,0},{4,5},{5,6},{6,7},{7,4},{8,9},{9,10},{10,1... | collective-permute-start | bytes 294920 | tf_op jit(solution)/shard_map/ppermute | solution.py:21
  94.1 2.6 copy-start.2
  96.8 2.8 copy-start.7
  124.7 2.2 copy-start.3
  126.9 3.0 copy-start.19
  126.9 4.4 %copy-start.18 = (s32[1024]{0:T(1024)S(1)}, s32[1024]{0:T(1024)}, u32[]{:S(2)}) copy-start(s32[1024]{0:T(1024)} %param.23) | copy-start | bytes 12292
  126.9 4.4 %copy-start.13 = (f32[4,1024]{1,0:T(4,128)S(1)}, f32[4,1024]{1,0:T(4,128)}, u32[]{:S(2)}) copy-start(f32[4,1024]{1,0:T(4,128)} %param.24) | copy-start | bytes 49156
  126.9 36.1 %copy-start.6 = (f32[4,32,16,128]{3,2,1,0:T(8,128)S(1)}, f32[4,32,16,128]{3,2,1,0:T(8,128)}, u32[]{:S(2)}) copy-start(f32[4,32,16,128]{3,2,1,0:T(8,128)} %param.18) | copy-start | bytes 3145732
  128.7 135.6 %all-reduce.2.cloned.1.call-start = ((), (), s32[]{:S(2)}) async-start(), calls=%async_computation | async-start | bytes 2097152 | tf_op jit(solution)/shard_map/psum | solution.py:176
  165.5 3.4 collective-permute-start.8
  169.7 13.2 %copy-start.8 = (bf16[1024,128]{1,0:T(8,128)(2,1)S(1)}, bf16[1024,128]{1,0:T(8,128)(2,1)}, u32[]{:S(2)}) copy-start(bf16[1024,128]{1,0:T(8,128)(2,1)} %param.25) | copy-start | bytes 786436
  170.0 14.3 %copy-start.10 = (f32[8,1024]{1,0:T(8,128)S(1)}, f32[8,1024]{1,0:T(8,128)}, u32[]{:S(2)}) copy-start(f32[8,1024]{1,0:T(8,128)} %param.27) | copy-start | bytes 98308
  170.0 14.3 %copy-start.11 = (f32[8,1024]{1,0:T(8,128)S(1)}, f32[8,1024]{1,0:T(8,128)}, u32[]{:S(2)}) copy-start(f32[8,1024]{1,0:T(8,128)} %param.26) | copy-start | bytes 98308
  170.0 14.3 %copy-start.12 = (f32[8,128]{1,0:T(8,128)S(1)}, f32[8,128]{1,0:T(8,128)}, u32[]{:S(2)}) copy-start(f32[8,128]{1,0:T(8,128)} %param.28) | copy-start | bytes 12292
  216.6 6.1 %collective-permute-start.9 = (f32[16,33,128]{2,0,1:T(8,128)S(1)}, f32[16,33,128]{2,0,1:T(8,128)S(1)}, u32[]{:S(2)}, u32[]{:S(2)}) collective-permute-start(f32[16,33,128]{2,0,1:T(8,128)S(1)} %slice.398), channel_id=1, source_target_pairs={{0,1},{1,2},{2,3},{3,0},{4,5},{5,6},{6,7},{7,4},{8,9},{9,10},{10,1... | collective-permute-start | bytes 811016 | tf_op jit(solution)/shard_map/ppermute | solution.py:33
  270.5 16.7 %collective-permute-start.10 = (f32[8,32,4,128]{3,1,2,0:T(8,128)S(1)}, f32[8,32,4,128]{3,1,2,0:T(8,128)S(1)}, u32[]{:S(2)}, u32[]{:S(2)}) collective-permute-start(f32[8,32,4,128]{3,1,2,0:T(8,128)S(1)} %get-tuple-element.31), channel_id=1, source_target_pairs={{0,4},{4,8},{8,12},{12,0},{1,5},{5,9},{9,13},{13,1},{2,6},{6,10},{... | collective-permute-start | bytes 1572872 | tf_op jit(solution)/shard_map/ppermute | solution.py:21
  272.0 24.5 %collective-permute-start.11 = (f32[8,32,4,128]{3,1,2,0:T(8,128)S(1)}, f32[8,32,4,128]{3,1,2,0:T(8,128)S(1)}, u32[]{:S(2)}, u32[]{:S(2)}) collective-permute-start(f32[8,32,4,128]{3,1,2,0:T(8,128)S(1)} %get-tuple-element.32), channel_id=1, source_target_pairs={{4,0},{8,4},{12,8},{0,12},{5,1},{9,5},{13,9},{1,13},{6,2},{10,6},{... | collective-permute-start | bytes 1572872 | tf_op jit(solution)/shard_map/ppermute | solution.py:23
  307.2 15.2 %collective-permute-start.13 = (f32[8,32,24,4]{1,2,3,0:T(8,128)}, f32[8,32,24,4]{1,2,3,0:T(8,128)}, u32[]{:S(2)}, u32[]{:S(2)}) collective-permute-start(f32[8,32,24,4]{1,2,3,0:T(8,128)} %copy.97), channel_id=1, source_target_pairs={{1,0},{2,1},{3,2},{0,3},{5,4},{6,5},{7,6},{4,7},{9,8},{10,9},{11,1... | collective-permute-start | bytes 294920 | tf_op jit(solution)/shard_map/ppermute | solution.py:23
  307.7 11.3 %collective-permute-start.12 = (f32[8,32,24,4]{1,2,3,0:T(8,128)}, f32[8,32,24,4]{1,2,3,0:T(8,128)}, u32[]{:S(2)}, u32[]{:S(2)}) collective-permute-start(f32[8,32,24,4]{1,2,3,0:T(8,128)} %copy.96), channel_id=1, source_target_pairs={{0,1},{1,2},{2,3},{3,0},{4,5},{5,6},{6,7},{7,4},{8,9},{9,10},{10,1... | collective-permute-start | bytes 294920 | tf_op jit(solution)/shard_map/ppermute | solution.py:21
  347.0 1.2 copy-start.5
  378.0 7.7 %copy-start.4 = (f32[8,32,16,128]{3,2,1,0:T(8,128)S(1)}, f32[8,32,16,128]{3,2,1,0:T(8,128)}, u32[]{:S(2)}) copy-start(f32[8,32,16,128]{3,2,1,0:T(8,128)} %param.16) | copy-start | bytes 6291460
  378.0 7.7 %copy-start.15 = (s32[32]{0:T(128)S(1)}, s32[32]{0:T(128)}, u32[]{:S(2)}) copy-start(s32[32]{0:T(128)} %copy-done.14) | copy-start | bytes 388
  378.0 7.7 %copy-start.17 = (s32[32]{0:T(128)S(1)}, s32[32]{0:T(128)}, u32[]{:S(2)}) copy-start(s32[32]{0:T(128)} %copy-done.16) | copy-start | bytes 388
  385.6 9.3 %copy-start.1 = (f32[4,32,32]{2,1,0:T(8,128)S(1)}, f32[4,32,32]{2,1,0:T(8,128)}, u32[]{:S(2)}) copy-start(f32[4,32,32]{2,1,0:T(8,128)} %param.21) | copy-start | bytes 49156
Sparse Core Ops, SparseCore 0:
  128.8 32.1 all-gather.2
  225.0 39.3 all-reduce.1
